TPU v7x, 512 devices: a whole 4x8x8 slice. The times are simulated.
512 devices in a mesh: drop: 16 (over z, core), freq: 32 (over x, y).
Axes of the slice: x: 4, y: 8, z: 8, core: 2. Of those that a mesh axis runs over, the one named last changes fastest.
Arguments:
- taps: float32 [32, 2, 23, 128], P('drop', None, None, 'freq'), may hold values from -6 to 6
- echo_lags: int32 [32, 23], P('drop'), may hold values from 0 to 319
- front_gain: float32 [4096], P('freq'), may hold values from 0.35 to 2, as said below
- symbols: int32 [32, 16, 4, 4096], P('drop', None, None, 'freq'), may hold values from 0 to 15
- noise: bfloat16 [32, 16, 2, 32, 4096], P('drop', None, None, None, 'freq'), may hold values from -6 to 6
- noise_std: float32 [32, 16], P('drop'), may hold values from 0.15 to 1.5
Outputs:
- detected: bfloat16 [32, 16, 2, 4, 4096], P('drop', None, None, None, 'freq')
- error_power: float32 [16], replicated
Inputs may be any that keep to these rules, and one draw needn't show every extreme that they name: `symbols`: 16-QAM indices. `front_gain`: positive front end amplitudes.
All inputs are finite; a program needn't handle non-finite values.
Results may differ from a plain program's by a relative error of at most 0.001.
Values sent between devices are 32-bit elements; how exact they have to be, the bound alone decides.
A program may use at most 64 MiB of HBM per device.

v0:
```python
import math

import jax
import jax.numpy as jnp
from jax import lax
from jax.sharding import PartitionSpec as P

RX = 32
TX = 4
FOURIER_POINTS = 4096


level_scale = 1.0 / math.sqrt(10.0)


def joined_along(parts, dim):
    parts = jnp.moveaxis(parts, 0, dim)
    shape = parts.shape
    return parts.reshape(*shape[:dim], shape[dim] * shape[dim + 1], *shape[dim + 2 :])


def sent_to_all(value, axis):
    peers = lax.axis_size(axis)
    return lax.all_to_all(
        jnp.broadcast_to(value[None], (peers, *value.shape)), axis, 0, 0, tiled=True
    )


def gather_directly(value, axis, dim):
    return joined_along(sent_to_all(value, axis), dim)


def of_everyone(value, axis):
    everything = sent_to_all(value, axis)
    return jnp.sum(everything, axis=0)


def packed_total(arrays, axis):
    ends = [0]
    for a in arrays:
        ends.append(ends[-1] + a.size)
    so_far = of_everyone(jnp.concatenate([a.ravel() for a in arrays]), axis)
    return tuple((so_far[b:e].reshape(a.shape) for a, b, e in zip(arrays, ends, ends[1:])))


def complex_mul(left_re, left_im, right_re, right_im):
    return (left_re * right_re - left_im * right_im, left_re * right_im + left_im * right_re)


def solve_small(gram_re, gram_im, rhs_re, rhs_im):
    streams = len(rhs_re)
    gram_re = [list(row) for row in gram_re]
    gram_im = [list(row) for row in gram_im]
    rhs_re = list(rhs_re)
    rhs_im = list(rhs_im)
    inverse = []
    for i in range(streams):
        pivot_inv = 1.0 / gram_re[i][i]
        inverse.append(pivot_inv)
        for j in range(i + 1, streams):
            factor_re = gram_re[j][i] * pivot_inv
            factor_im = gram_im[j][i] * pivot_inv
            for k in range(i + 1, streams):
                prod_re, prod_im = complex_mul(factor_re, factor_im, gram_re[i][k], gram_im[i][k])
                gram_re[j][k] = gram_re[j][k] - prod_re
                gram_im[j][k] = gram_im[j][k] - prod_im
            prod_re, prod_im = complex_mul(factor_re, factor_im, rhs_re[i], rhs_im[i])
            rhs_re[j] = rhs_re[j] - prod_re
            rhs_im[j] = rhs_im[j] - prod_im
    result_re = [None] * streams
    result_im = [None] * streams
    for i in reversed(range(streams)):
        partial_re, partial_im = (rhs_re[i], rhs_im[i])
        for k in range(i + 1, streams):
            prod_re, prod_im = complex_mul(gram_re[i][k], gram_im[i][k], result_re[k], result_im[k])
            partial_re = partial_re - prod_re
            partial_im = partial_im - prod_im
        result_re[i] = partial_re * inverse[i]
        result_im[i] = partial_im * inverse[i]
    return (result_re, result_im)


def spectral_gain(echo_coefficients, echo_lags, tone_positions):
    highest = lax.Precision.HIGHEST
    rotation_cycles = echo_lags[:, :, None] * tone_positions[None, None, :] % FOURIER_POINTS
    angle = rotation_cycles.astype(jnp.float32) * (2.0 * math.pi / FOURIER_POINTS)
    cosine = jnp.cos(angle)
    sine = jnp.sin(angle)
    resp_re = jnp.einsum(
        "dlj,dlk->djk", echo_coefficients[:, 0], cosine, precision=highest
    ) + jnp.einsum("dlj,dlk->djk", echo_coefficients[:, 1], sine, precision=highest)
    resp_im = jnp.einsum(
        "dlj,dlk->djk", echo_coefficients[:, 1], cosine, precision=highest
    ) - jnp.einsum("dlj,dlk->djk", echo_coefficients[:, 0], sine, precision=highest)
    return jnp.stack([resp_re, resp_im], 1)


def detect(chan_re, chan_im, rhs_re, rhs_im):
    highest = lax.Precision.HIGHEST
    gram_re = jnp.einsum("drtk,druk->dtuk", chan_re, chan_re, precision=highest) + jnp.einsum(
        "drtk,druk->dtuk", chan_im, chan_im, precision=highest
    )
    gram_im = jnp.einsum("drtk,druk->dtuk", chan_re, chan_im, precision=highest) - jnp.einsum(
        "drtk,druk->dtuk", chan_im, chan_re, precision=highest
    )
    match_re = jnp.einsum("drtk,dsrk->dstk", chan_re, rhs_re, precision=highest) + jnp.einsum(
        "drtk,dsrk->dstk", chan_im, rhs_im, precision=highest
    )
    match_im = jnp.einsum("drtk,dsrk->dstk", chan_re, rhs_im, precision=highest) - jnp.einsum(
        "drtk,dsrk->dstk", chan_im, rhs_re, precision=highest
    )
    streams = chan_re.shape[2]
    entries_re = [[gram_re[:, t, u][:, None] for u in range(streams)] for t in range(streams)]
    entries_im = [[gram_im[:, t, u][:, None] for u in range(streams)] for t in range(streams)]
    result_re, result_im = solve_small(
        entries_re,
        entries_im,
        [match_re[:, :, t] for t in range(streams)],
        [match_im[:, :, t] for t in range(streams)],
    )
    return (jnp.stack(result_re, 2), jnp.stack(result_im, 2))


def shards(taps, echo_lags, front_gain, symbols, noise, noise_std):
    drop_dev = taps.shape[0]
    sc_dev = front_gain.shape[0]
    gathered = gather_directly(taps, "freq", 3)
    tone_positions = lax.axis_index("freq") * sc_dev + jnp.arange(sc_dev, dtype=jnp.int32)
    response = spectral_gain(gathered, echo_lags, tone_positions)
    response = response * front_gain[None, None, None, :]
    power_part = jnp.sum(response * response, axis=(1, 2, 3))
    sent_re = (2 * (symbols % 4) - 3).astype(jnp.float32) * level_scale
    sent_im = (2 * (symbols // 4) - 3).astype(jnp.float32) * level_scale
    noise_re = noise[:, :, 0].astype(jnp.float32)
    noise_im = noise[:, :, 1].astype(jnp.float32)
    drops_all = drop_dev * lax.axis_size("drop")
    norm_count = FOURIER_POINTS * RX * TX
    chan_re = response[:, 0].reshape(drop_dev, RX, TX, sc_dev)
    chan_im = response[:, 1].reshape(drop_dev, RX, TX, sc_dev)
    weight_re, weight_im = detect(chan_re, chan_im, noise_re, noise_im)
    raw_terms = (
        noise_std * noise_std * jnp.sum(weight_re * weight_re + weight_im * weight_im, axis=(2, 3))
    )
    power_sum, raw_sum = packed_total((power_part, raw_terms), "freq")
    power = power_sum / norm_count
    drop_errors = power[:, None] * raw_sum
    total = of_everyone(jnp.sum(drop_errors, axis=0), "drop")
    amplitude = (noise_std * jnp.sqrt(power)[:, None])[:, :, None, None]
    estimate_re = sent_re + amplitude * weight_re
    estimate_im = sent_im + amplitude * weight_im
    detected = jnp.stack([estimate_re, estimate_im], 2).astype(jnp.bfloat16)
    error_power = RX * total / (drops_all * TX * FOURIER_POINTS)
    return (detected, error_power)


def solution(mesh):
    placed = (
        P("drop", None, None, "freq"),
        P("drop", None),
        P("freq"),
        P("drop", None, None, "freq"),
        P("drop", None, None, None, "freq"),
        P("drop", None),
    )
    return jax.shard_map(
        shards,
        mesh=mesh,
        in_specs=placed,
        out_specs=(P("drop", None, None, None, "freq"), P()),
        check_vma=False,
    )
```

profile of v0, /device:TPU:1, one launch (start us, length us, event | category | flops | bytes accessed | tf_op | source)
XLA Modules:
  0.0 104.8 jit_solution(8558947325879997509)
XLA Ops:
  0.7 0.7 copy-done
  1.4 0.9 reshape.1214
  2.3 10.5 %all-to-all-start = ((f32[32,1,368]{2,1,0:T(1,128)}), f32[32,1,368]{2,1,0:T(1,128)S(1)}, u32[]{:S(2)}, u32[]{:S(2)}) async-start(f32[32,1,368]{2,1,0:T(1,128)} %reshape.1214), calls=%async_computation | async-start | bytes 98304 | tf_op jit(solution)/shard_map/all_to_all | solution.py:24
  12.9 0.8 copy.938
  13.7 0.8 copy.940
  14.5 7.1 %all-to-all-done = f32[32,1,368]{2,1,0:T(1,128)S(1)} async-done(((f32[32,1,368]{2,1,0:T(1,128)}), f32[32,1,368]{2,1,0:T(1,128)S(1)}, u32[]{:S(2)}, u32[]{:S(2)}) %all-to-all-start) | async-done | bytes 47136 | tf_op jit(solution)/shard_map/all_to_all | solution.py:24
  21.6 0.5 broadcast.527
  22.1 0.8 reduce.58
  22.9 0.4 reshape.1215
  23.3 0.7 copy-done.5
  24.0 0.4 fusion.14
  24.4 0.4 fusion.13
  24.9 0.4 fusion.2
  25.3 0.4 fusion.3
  26.6 1.8 %fusion.69 = f32[2,128,4,4]{3,2,1,0:T(4,128)S(1)} fusion(f32[2,32,4,128]{1,2,3,0:T(4,128)S(1)} %copy.939), kind=kOutput, calls=%fused_computation.153 | convolution fusion | flops 1572864 | bytes 147456 | tf_op jit(solution)/shard_map/drtk,druk->dtuk/dot_general | solution.py:100
  28.4 1.8 %fusion.70 = f32[2,128,4,4]{3,2,1,0:T(4,128)S(1)} fusion(f32[2,32,4,128]{1,2,3,0:T(4,128)S(1)} %copy.941, f32[2,32,4,128]{1,2,3,0:T(4,128)S(1)} %copy.939), kind=kOutput, calls=%fused_computation.154 | convolution fusion | flops 1572864 | bytes 278528 | tf_op jit(solution)/shard_map/drtk,druk->dtuk/dot_general | solution.py:103
  30.2 2.5 %fusion.8 = f32[2,128,4,16]{3,2,1,0:T(4,128)} fusion(f32[2,32,4,128]{1,2,3,0:T(4,128)S(1)} %copy.941, bf16[2,16,1,32,128]{3,1,4,0,2:T(8,128)(2,1)S(1)} %copy.938), kind=kOutput, calls=%fused_computation.12 | convolution fusion | flops 6291456 | bytes 458752 | tf_op jit(solution)/shard_map/drtk,dsrk->dstk/dot_general | solution.py:109
  32.7 2.6 %fusion.10 = f32[2,128,4,16]{3,2,1,0:T(4,128)} fusion(f32[2,32,4,128]{1,2,3,0:T(4,128)S(1)} %copy.939, bf16[2,16,1,32,128]{3,1,4,0,2:T(8,128)(2,1)S(1)} %copy.938), kind=kOutput, calls=%fused_computation.14 | convolution fusion | flops 6291456 | bytes 458752 | tf_op jit(solution)/shard_map/drtk,dsrk->dstk/dot_general | solution.py:106
  35.3 1.8 %fusion.4 = f32[2,128,4,16]{3,2,1,0:T(4,128)S(1)} fusion(f32[2,32,4,128]{1,2,3,0:T(4,128)S(1)} %copy.939, bf16[2,16,1,32,128]{3,1,4,0,2:T(8,128)(2,1)S(1)} %copy.940), kind=kOutput, calls=%fused_computation.8 | convolution fusion | flops 6291456 | bytes 458752 | tf_op jit(solution)/shard_map/drtk,dsrk->dstk/dot_general | solution.py:109
  37.1 1.9 %fusion.6 = f32[2,128,4,16]{3,2,1,0:T(4,128)S(1)} fusion(f32[2,32,4,128]{1,2,3,0:T(4,128)S(1)} %copy.941, bf16[2,16,1,32,128]{3,1,4,0,2:T(8,128)(2,1)S(1)} %copy.940), kind=kOutput, calls=%fused_computation.10 | convolution fusion | flops 6291456 | bytes 458752 | tf_op jit(solution)/shard_map/drtk,dsrk->dstk/dot_general | solution.py:106
  39.0 1.9 %fusion = f32[2,4,4,128]{1,2,3,0:T(4,128)S(1)} fusion(f32[2,128,4,4]{3,2,1,0:T(4,128)S(1)} %fusion.70, f32[2,32,4,128]{1,2,3,0:T(4,128)S(1)} %copy.939, f32[2,32,4,128]{1,2,3,0:T(4,128)S(1)} %copy.941), kind=kOutput, calls=%fused_computation.1 | convolution fusion | flops 1576960 | bytes 294912 | tf_op jit(solution)/shard_map/drtk,druk->dtuk/dot_general | solution.py:103
  40.9 11.0 %slice_reduce_fusion = (f32[2,128]{1,0:T(2,128)S(1)}, f32[2,128]{1,0:T(2,128)S(1)}, f32[2,128]{1,0:T(2,128)S(1)}, f32[2,128]{1,0:T(2,128)S(1)}, f32[2,128]{1,0:T...) fusion(f32[2,4,4,128]{1,2,3,0:T(4,128)S(1)} %fusion), kind=kLoop, calls=%fused_computation.18 | loop fusion | bytes 24576 | tf_op jit(solution)/shard_map/slice | solution.py:114
  51.9 2.0 %fusion.1 = f32[2,4,4,128]{1,2,3,0:T(4,128)S(1)} fusion(f32[2,128,4,4]{3,2,1,0:T(4,128)S(1)} %fusion.69, f32[2,32,4,128]{1,2,3,0:T(4,128)S(1)} %copy.941), kind=kOutput, calls=%fused_computation.3 | convolution fusion | flops 1576960 | bytes 163840 | tf_op jit(solution)/shard_map/drtk,druk->dtuk/dot_general | solution.py:100
  53.9 14.3 %slice_reduce_fusion.1 = (f32[2,128]{1,0:T(2,128)S(1)}, f32[2,128]{1,0:T(2,128)S(1)}, f32[2,128]{1,0:T(2,128)S(1)}, f32[2,128]{1,0:T(2,128)S(1)}, f32[2,128]{1,0...) fusion(f32[2,4,4,128]{1,2,3,0:T(4,128)S(1)} %fusion.1), kind=kLoop, calls=%fused_computation.19 | loop fusion | flops 256 | bytes 32768 | tf_op jit(solution)/shard_map/slice | solution.py:113
  68.5 0.9 copy-done.1
  70.2 0.6 copy-done.6
  71.0 11.7 %all_to_all.17 = f32[32,1,34]{2,1,0:T(1,128)S(1)} all-to-all(f32[32,1,34]{2,1,0:T(1,128)S(1)} %broadcast_in_dim.7), channel_id=1, replica_groups=mesh['drop'=16,'freq'=32] {'freq'}, dimensions={0} | all-to-all | bytes 8704 | tf_op jit(solution)/shard_map/all_to_all | solution.py:24
  83.0 0.6 broadcast_in_dim.8
  83.6 13.6 %all-to-all-start.2 = ((f32[16,1,16]{2,1,0:T(1,128)}), f32[16,1,16]{2,1,0:T(1,128)S(1)}, u32[]{:S(2)}, u32[]{:S(2)}) async-start(f32[16,1,16]{2,1,0:T(1,128)} %broadcast_in_dim.8), calls=%async_computation.2 | async-start | bytes 16384 | tf_op jit(solution)/shard_map/all_to_all | solution.py:24
  97.3 0.7 copy.961
  98.0 6.3 %all-to-all-done.2 = f32[16,1,16]{2,1,0:T(1,128)S(1)} async-done(((f32[16,1,16]{2,1,0:T(1,128)}), f32[16,1,16]{2,1,0:T(1,128)S(1)}, u32[]{:S(2)}, u32[]{:S(2)}) %all-to-all-start.2) | async-done | bytes 1056 | tf_op jit(solution)/shard_map/all_to_all | solution.py:24
  104.3 0.5 broadcast_multiply_fusion.1
  (44 shorter events, 2.7 us)
Async XLA Ops:
  0.6 0.7 copy-start
  0.6 12.2 %copy-start.3 = (bf16[2,16,2,32,128]{4,3,2,1,0:T(8,128)(2,1)S(1)}, bf16[2,16,2,32,128]{4,3,2,1,0:T(8,128)(2,1)}, u32[]{:S(2)}) copy-start(bf16[2,16,2,32,128]{4,3,2,1,0:T(8,128)(2,1)} %param.10) | copy-start | bytes 1572868
  2.3 19.3 %all-to-all-start = ((f32[32,1,368]{2,1,0:T(1,128)}), f32[32,1,368]{2,1,0:T(1,128)S(1)}, u32[]{:S(2)}, u32[]{:S(2)}) async-start(f32[32,1,368]{2,1,0:T(1,128)} %reshape.1214), calls=%async_computation | async-start | bytes 98304 | tf_op jit(solution)/shard_map/all_to_all | solution.py:24
  23.3 0.7 copy-start.5
  25.3 0.7 copy-start.7
  53.9 14.4 %copy-start.2 = (f32[2,128,4,16]{3,2,1,0:T(4,128)S(1)}, f32[2,128,4,16]{3,2,1,0:T(4,128)}, u32[]{:S(2)}) copy-start(f32[2,128,4,16]{3,2,1,0:T(4,128)} %fusion.10) | copy-start | bytes 196612
  68.3 1.0 copy-start.1
  70.1 0.7 copy-start.6
  70.8 26.4 %copy-start.4 = (s32[2,16,4,128]{3,2,1,0:T(4,128)S(1)}, s32[2,16,4,128]{3,2,1,0:T(4,128)}, u32[]{:S(2)}) copy-start(s32[2,16,4,128]{3,2,1,0:T(4,128)} %param.9) | copy-start | bytes 196612
  83.6 20.6 %all-to-all-start.2 = ((f32[16,1,16]{2,1,0:T(1,128)}), f32[16,1,16]{2,1,0:T(1,128)S(1)}, u32[]{:S(2)}, u32[]{:S(2)}) async-start(f32[16,1,16]{2,1,0:T(1,128)} %broadcast_in_dim.8), calls=%async_computation.2 | async-start | bytes 16384 | tf_op jit(solution)/shard_map/all_to_all | solution.py:24
where the time goes:
time: 105 us
  starting transfers between devices  24.1 us (23%)
  local copies, waits for them, and re-layouts  20.3 us (19%)
  matrix products  17.9 us (17%)
  other arithmetic  16.5 us (16%)
  waiting for transfers between devices  13.4 us (13%)
  blocking collectives  11.7 us (11%)
    all_to_all x2, starting transfers between devices, sent_to_all(): lax.all_to_all(jnp.broadcast_to(value[None], (peers, *value.shape)), axis...  24.1 us
    slice x1, other arithmetic, detect(): gram_re[:, t, u][:, None]  14.3 us
    all_to_all x2, waiting for transfers between devices, sent_to_all(): lax.all_to_all(jnp.broadcast_to(value[None], (peers, *value.shape)), axis...  13.4 us
    all_to_all x1, blocking collectives, sent_to_all(): lax.all_to_all(jnp.broadcast_to(value[None], (peers, *value.shape)), axis...  11.7 us
    slice x1, local copies, waits for them, and re-layouts, detect(): gram_im[:, t, u][:, None]  11 us
    unnamed x20, local copies, waits for them, and re-layouts  5.03 us
    dot_general x1, matrix products, detect(): jnp.einsum('drtk,dsrk->dstk', chan_re, rhs_re, precision=highest)  2.57 us
    dot_general x1, matrix products, detect(): jnp.einsum('drtk,dsrk->dstk', chan_im, rhs_re, precision=highest)  2.55 us
  transfers between devices with their start and end apart: 2, of which 2 were waited for; matrix products, arithmetic and copies ran while one was open for 2% of the time, Pallas kernels for 0%

commit v1 on v0

v1 whole, which is shorter than its diff:
```python
import math

import jax
import jax.numpy as jnp
from jax import lax
from jax.experimental import pallas as pl
from jax.experimental.pallas import tpu as pltpu
from jax.sharding import PartitionSpec as P

RX = 32
TX = 4
TAPS = 23
SNRS = 16
FOURIER_POINTS = 4096
DROPS = 32
LANES = 128
MESH = pl.DeviceIdType.MESH
F32 = jnp.float32

level_scale = 1.0 / math.sqrt(10.0)


def cos_sin(cycles):
    shifted = cycles + 512
    quadrant = lax.shift_right_logical(shifted, 10) & 3
    x = ((shifted & 1023) - 512).astype(F32) * (2.0 * math.pi / FOURIER_POINTS)
    x2 = x * x
    s = x * (1.0 + x2 * (-1 / 6 + x2 * (1 / 120 + x2 * (-1 / 5040 + x2 * (1 / 362880)))))
    c = 1.0 + x2 * (-0.5 + x2 * (1 / 24 + x2 * (-1 / 720 + x2 * (1 / 40320 + x2 * (-1 / 3628800)))))
    odd = (quadrant & 1) == 1
    cosine = jnp.where(odd, s, c)
    sine = jnp.where(odd, c, s)
    cosine = jnp.where((quadrant == 1) | (quadrant == 2), -cosine, cosine)
    sine = jnp.where(quadrant >= 2, -sine, sine)
    return cosine, sine


def over_sublanes(x):
    x = (x[0:8] + x[8:16]) + (x[16:24] + x[24:32])
    x = x + pltpu.roll(x, 4, 0)
    x = x + pltpu.roll(x, 2, 0)
    return x + pltpu.roll(x, 1, 0)


def cmul(a, b):
    return a[0] * b[0] - a[1] * b[1], a[0] * b[1] + a[1] * b[0]


def cmul_conj(a, b):
    return a[0] * b[0] + a[1] * b[1], a[0] * b[1] - a[1] * b[0]


def csub(a, b):
    return a[0] - b[0], a[1] - b[1]


def kernel(
    taps_hbm, lags_hbm, gain_hbm, symbols_hbm, noise_hbm, std_hbm,
    detected_ref, error_ref,
    taps_v, lags_v, gain_v, symbols_v, noise_v, std_v,
    packed, padded, column, gathered, table, channel, noise_f, out_f, row_send, rows, sum_send, sums,
    in_sems, send_sems, recv_sems,
):
    n_freq, n_drop = lax.axis_size("freq"), lax.axis_size("drop")
    freq, drop = lax.axis_index("freq"), lax.axis_index("drop")
    barrier = pltpu.get_barrier_semaphore()

    def freq_peer(i):
        return {"freq": lax.rem(freq + i, n_freq)}

    def drop_peer(i):
        return {"drop": lax.rem(drop + i, n_drop)}

    @pl.loop(1, n_freq)
    def _(i):
        pl.semaphore_signal(barrier, inc=1, device_id=freq_peer(i), device_id_type=MESH)

    @pl.loop(1, n_drop)
    def _(i):
        pl.semaphore_signal(barrier, inc=1, device_id=drop_peer(i), device_id_type=MESH)

    loads = [
        pltpu.make_async_copy(src, dst, in_sems.at[i])
        for i, (src, dst) in enumerate(
            (
                (taps_hbm, taps_v), (lags_hbm, lags_v), (gain_hbm, gain_v),
                (symbols_hbm, symbols_v), (noise_hbm, noise_v), (std_hbm, std_v),
            )
        )
    ]
    for load in loads:
        load.start()

    padded[...] = jnp.zeros_like(padded)
    loads[0].wait()
    for q in range(4):
        padded[q, :, 0:TAPS] = taps_v[q // 2, q % 2]
    own = padded[0]
    for q in range(1, 4):
        own = own + pltpu.roll(padded[q], 32 * q, 1)
    packed[...] = own
    gathered[freq] = own

    pl.semaphore_wait(barrier, n_freq + n_drop - 2)

    def send_taps(i):
        return pltpu.make_async_remote_copy(
            src_ref=packed, dst_ref=gathered.at[freq], send_sem=send_sems.at[0], recv_sem=recv_sems.at[0],
            device_id=freq_peer(i), device_id_type=MESH,
        )

    @pl.loop(1, n_freq)
    def _(i):
        send_taps(i).start()

    loads[1].wait()
    loads[2].wait()
    loads[5].wait()
    column[...] = jnp.zeros_like(column)
    column[0:2, 0:TAPS] = lags_v[...].astype(F32)
    column[2:4, 0:SNRS] = std_v[...]
    turned = jnp.transpose(column[...])
    gain = gain_v[...]
    tone = freq * LANES + lax.broadcasted_iota(jnp.int32, (32, LANES), 1)
    table[...] = jnp.zeros_like(table)
    for d in range(2):
        lag = turned[0:32, d : d + 1].astype(jnp.int32)
        cosine, sine = cos_sin((lag * tone) & (FOURIER_POINTS - 1))
        cosine = cosine * gain
        sine = sine * gain
        table[64 * d : 64 * d + 32, 256 * d : 256 * d + 128] = cosine
        table[64 * d + 32 : 64 * d + 64, 256 * d : 256 * d + 128] = sine
        table[64 * d : 64 * d + 32, 256 * d + 128 : 256 * d + 256] = -sine
        table[64 * d + 32 : 64 * d + 64, 256 * d + 128 : 256 * d + 256] = cosine
    std = [jnp.broadcast_to(turned[0:SNRS, 2 + d : 3 + d], (SNRS, LANES)).reshape(2, 8, LANES) for d in range(2)]

    loads[4].wait()

    @pl.loop(0, 32)
    def _(i):
        at = pl.ds(pl.multiple_of(i * 64, 64), 64)
        noise_f[at, :] = noise_v[at, :].astype(F32)

    pltpu.make_async_remote_copy(
        src_ref=gathered.at[pl.ds(0, n_freq - 1)], dst_ref=gathered.at[pl.ds(0, n_freq - 1)],
        send_sem=send_sems.at[0], recv_sem=recv_sems.at[0], device_id=freq_peer(1), device_id_type=MESH,
    ).wait_recv()
    response = jnp.dot(
        gathered[...].reshape(RX * TX, LANES), table[...],
        precision=lax.Precision.HIGHEST, preferred_element_type=F32,
    )
    for q in range(4):
        channel[q] = response[:, LANES * q : LANES * (q + 1)]

    def match_step(r, so_far):
        result = []
        for d in range(2):
            noise = [noise_f[pl.ds(1024 * d + 32 * c + r, SNRS, stride=64), :].reshape(2, 8, LANES) for c in range(2)]
            for t in range(TX):
                h = [channel[2 * d + c, pl.ds(TX * r + t, 1), :] for c in range(2)]
                h = [jnp.broadcast_to(v, (8, LANES))[None] for v in h]
                re, im = cmul_conj(h, noise)
                old_re, old_im = so_far[4 * d + t]
                result.append((old_re + re, old_im + im))
        return tuple(result)

    nothing = jnp.zeros((2, 8, LANES), F32)
    match = lax.fori_loop(0, RX, match_step, ((nothing, nothing),) * 8, unroll=4)

    solved, totals, powers = [], [], []
    for d in range(2):
        h = [[channel[2 * d + c, pl.ds(t, RX, stride=TX), :] for c in range(2)] for t in range(TX)]
        diagonal = [over_sublanes(h[t][0] * h[t][0] + h[t][1] * h[t][1]) for t in range(TX)]
        upper = {}
        for t in range(TX):
            for u in range(t + 1, TX):
                re, im = cmul_conj(h[t], h[u])
                upper[t, u] = over_sublanes(re), over_sublanes(im)
        powers.append((diagonal[0] + diagonal[1]) + (diagonal[2] + diagonal[3]))
        right = [match[4 * d + t] for t in range(TX)]
        inverse = []
        for i in range(TX):
            inverse.append(1.0 / diagonal[i])
            for j in range(i + 1, TX):
                factor = upper[i, j][0] * inverse[i], -upper[i, j][1] * inverse[i]
                diagonal[j] = diagonal[j] - (factor[0] * upper[i, j][0] - factor[1] * upper[i, j][1])
                for k in range(j + 1, TX):
                    upper[j, k] = csub(upper[j, k], cmul(factor, upper[i, k]))
                right[j] = csub(right[j], cmul(factor, right[i]))
        result = [None] * TX
        for i in reversed(range(TX)):
            partial = right[i]
            for k in range(i + 1, TX):
                partial = csub(partial, cmul(upper[i, k], result[k]))
            result[i] = partial[0] * inverse[i], partial[1] * inverse[i]
        solved.append(result)
        total = result[0][0] * result[0][0] + result[0][1] * result[0][1]
        for t in range(1, TX):
            total = total + result[t][0] * result[t][0] + result[t][1] * result[t][1]
        totals.append(total * (std[d] * std[d]))

    lane8 = lax.broadcasted_iota(jnp.int32, (8, LANES), 1)
    sub8 = lax.broadcasted_iota(jnp.int32, (8, LANES), 0)
    power_rows = jnp.where(sub8 == 0, powers[0], jnp.where(sub8 == 1, powers[1], 0.0))
    stacked = [totals[0][0], totals[0][1], totals[1][0], totals[1][1], power_rows]
    row = jnp.zeros((8, LANES), F32)
    for i, piece in enumerate(stacked):
        row = row + jnp.where(lane8 == sub8 + 8 * i, jnp.sum(piece, axis=1, keepdims=True), 0.0)
    row = jnp.sum(row, axis=0, keepdims=True)
    row_send[...] = row
    rows[freq] = row

    def send_row(i):
        return pltpu.make_async_remote_copy(
            src_ref=row_send, dst_ref=rows.at[freq], send_sem=send_sems.at[1], recv_sem=recv_sems.at[1],
            device_id=freq_peer(i), device_id_type=MESH,
        )

    @pl.loop(1, n_freq)
    def _(i):
        send_row(i).start()

    loads[3].wait()
    sent = []
    for d in range(2):
        for t in range(TX):
            symbol = symbols_v[pl.ds(64 * d + t, SNRS, stride=TX), :]
            sent.append(
                (
                    (2 * (symbol & 3) - 3).astype(F32) * level_scale,
                    (2 * lax.shift_right_logical(symbol, 2) - 3).astype(F32) * level_scale,
                )
            )

    def all_rows(ref, n, i):
        pltpu.make_async_remote_copy(
            src_ref=ref.at[pl.ds(0, n - 1)], dst_ref=ref.at[pl.ds(0, n - 1)],
            send_sem=send_sems.at[i], recv_sem=recv_sems.at[i], device_id=freq_peer(1), device_id_type=MESH,
        ).wait_recv()
        return jnp.sum(ref[...], axis=0)

    row = all_rows(rows, n_freq, 1)
    lane = lax.broadcasted_iota(jnp.int32, (1, LANES), 1)
    power = [
        jnp.sum(jnp.where(lane == 32 + d, row, 0.0), axis=1, keepdims=True) * (1.0 / (FOURIER_POINTS * RX * TX))
        for d in range(2)
    ]
    weighted = row * jnp.where(lane < SNRS, power[0], jnp.where(lane < 2 * SNRS, power[1], 0.0))
    sum_send[...] = weighted
    sums[drop] = weighted

    def send_sum(i):
        return pltpu.make_async_remote_copy(
            src_ref=sum_send, dst_ref=sums.at[drop], send_sem=send_sems.at[2], recv_sem=recv_sems.at[2],
            device_id=drop_peer(i), device_id_type=MESH,
        )

    @pl.loop(1, n_drop)
    def _(i):
        send_sum(i).start()

    for d in range(2):
        amplitude = std[d] * jnp.sqrt(jnp.broadcast_to(power[d], (8, LANES)))
        for t in range(TX):
            for c in range(2):
                estimate = sent[4 * d + t][c] + (amplitude * solved[d][t][c]).reshape(SNRS, LANES)
                out_f[pl.ds(128 * d + 4 * c + t, SNRS, stride=8), :] = estimate
    detected_ref[...] = out_f[...].astype(jnp.bfloat16)

    total = all_rows(sums, n_drop, 2)
    total = total[:, 0:SNRS] + total[:, SNRS : 2 * SNRS]
    error_ref[...] = RX * total / (DROPS * TX * FOURIER_POINTS)

    for i, (ref, n) in enumerate(((gathered, n_freq), (rows, n_freq), (sums, n_drop))):
        pltpu.make_async_remote_copy(
            src_ref=ref.at[pl.ds(0, n - 1)], dst_ref=ref.at[pl.ds(0, n - 1)],
            send_sem=send_sems.at[i], recv_sem=recv_sems.at[i], device_id=freq_peer(1), device_id_type=MESH,
        ).wait_send()


def shards(taps, echo_lags, front_gain, symbols, noise, noise_std):
    n_freq, n_drop = lax.axis_size("freq"), lax.axis_size("drop")
    vmem = pltpu.VMEM
    detected, error = pl.pallas_call(
        kernel,
        out_shape=(
            jax.ShapeDtypeStruct((2 * SNRS * 8, LANES), jnp.bfloat16),
            jax.ShapeDtypeStruct((1, SNRS), F32),
        ),
        in_specs=[pl.BlockSpec(memory_space=pltpu.HBM)] * 6,
        out_specs=(pl.BlockSpec(memory_space=pltpu.VMEM), pl.BlockSpec(memory_space=pltpu.VMEM)),
        scratch_shapes=[
            vmem((2, 2, TX, TAPS), F32),
            vmem((2, TAPS), jnp.int32),
            vmem((1, LANES), F32),
            vmem((2 * SNRS * TX, LANES), jnp.int32),
            vmem((2 * SNRS * 2 * RX, LANES), jnp.bfloat16),
            vmem((2, SNRS), F32),
            vmem((TX, LANES), F32),
            vmem((4, TX, LANES), F32),
            vmem((LANES, LANES), F32),
            vmem((n_freq, TX, LANES), F32),
            vmem((LANES, 4 * LANES), F32),
            vmem((4, RX * TX, LANES), F32),
            vmem((2 * SNRS * 2 * RX, LANES), F32),
            vmem((2 * SNRS * 8, LANES), F32),
            vmem((1, LANES), F32),
            vmem((n_freq, 1, LANES), F32),
            vmem((1, LANES), F32),
            vmem((n_drop, 1, LANES), F32),
            pltpu.SemaphoreType.DMA((6,)),
            pltpu.SemaphoreType.DMA((3,)),
            pltpu.SemaphoreType.DMA((3,)),
        ],
        compiler_params=pltpu.CompilerParams(collective_id=0, has_side_effects=True),
    )(
        jnp.transpose(taps, (0, 1, 3, 2)),
        echo_lags,
        front_gain.reshape(1, LANES),
        symbols.reshape(2 * SNRS * TX, LANES),
        noise.reshape(2 * SNRS * 2 * RX, LANES),
        noise_std,
    )
    return detected.reshape(2, SNRS, 2, TX, LANES), error.reshape(SNRS)


def solution(mesh):
    placed = (
        P("drop", None, None, "freq"),
        P("drop", None),
        P("freq"),
        P("drop", None, None, "freq"),
        P("drop", None, None, None, "freq"),
        P("drop", None),
    )
    return jax.shard_map(
        shards,
        mesh=mesh,
        in_specs=placed,
        out_specs=(P("drop", None, None, None, "freq"), P()),
        check_vma=False,
    )
```

time: 105 us -> 38.2 us (0.36)
  Pallas kernels: 0 us -> 35.3 us
  starting transfers between devices: 24.1 us -> 0 us
  local copies, waits for them, and re-layouts: 20.3 us -> 2.01 us
  matrix products: 17.9 us -> 0 us
  other arithmetic: 16.5 us -> 0 us
  waiting for transfers between devices: 13.4 us -> 0 us
  blocking collectives: 11.7 us -> 0 us
    pallas_call x0 -> x1, Pallas kernels: none -> 35.3 us  [shards(): pl.pallas_call(kernel, out_shape=(jax.ShapeDtypeStruct((2 * SNRS * 8, LAN...]
    all_to_all x2 -> x0, starting transfers between devices: 24.1 us -> none  [sent_to_all(): lax.all_to_all(jnp.broadcast_to(value[None], (peers, *value.shape)), axis...]
    dot_general x12 -> x0, matrix products: 17.9 us -> none  [the longest x1 2.57 us: detect(): jnp.einsum('drtk,dsrk->dstk', chan_re, rhs_re, precision=highest)]
    slice x1 -> x0, other arithmetic: 14.3 us -> none  [detect(): gram_re[:, t, u][:, None]]
    all_to_all x2 -> x0, waiting for transfers between devices: 13.4 us -> none  [sent_to_all(): lax.all_to_all(jnp.broadcast_to(value[None], (peers, *value.shape)), axis...]
    slice x6 -> x0, local copies, waits for them, and re-layouts: 12.7 us -> none  [the longest x1 11 us: detect(): gram_im[:, t, u][:, None]]
    all_to_all x1 -> x0, blocking collectives: 11.7 us -> none  [sent_to_all(): lax.all_to_all(jnp.broadcast_to(value[None], (peers, *value.shape)), axis...]
    unnamed x20 -> x4, local copies, waits for them, and re-layouts: 5.03 us -> 2.01 us
  transfers between devices with their start and end apart: 2 -> 0, of which waited for: 2 -> 0; matrix products, arithmetic and copies ran while one was open for 2% -> 0% of each run, Pallas kernels for 0% -> 0%
where the time goes in v1:
time: 38.2 us; the launch traced here: 38 us
  Pallas kernels  35.3 us (92%)
  local copies, waits for them, and re-layouts  2.01 us (5%)
  between operations  0.65 us (2%)
    pallas_call x1, Pallas kernels, shards(): pl.pallas_call(kernel, out_shape=(jax.ShapeDtypeStruct((2 * SNRS * 8, LAN...  35.3 us
    unnamed x4, local copies, waits for them, and re-layouts  2.01 us

profile of v1, /device:TPU:1, one launch (start us, length us, event | category | flops | bytes accessed | tf_op | source)
XLA Modules:
  0.0 38.0 jit_solution(7734536517176223603)
XLA Ops:
  0.6 35.3 %shard_map.77 = (bf16[256,128]{1,0:T(8,128)(2,1)}, f32[1,16]{1,0:T(1,128)}) custom-call(f32[2,2,4,23]{3,2,1,0:T(4,128)} %bitcast.9, s32[2,23]{1,0:T(2,128)} %lags_hbm.1, f32[1,128]{1,0:T(1,128)} %bitcast.10, s32[128,128]{1,0:T(8,128)} %bitcast.8, bf16[2048,128]{1,0:T(8,128)(2,1)} %bitcast.6, f32[2,16]{1,0:T(2,128)} %std_hbm.1), custom_call_target="tpu_custom_call" | custom-call | tf_op jit(solution)/shard_map/pallas_call | solution.py:284
  36.0 0.0 copy-start
  36.0 1.5 %copy.10 = bf16[2,16,2,4,128]{4,3,2,1,0:T(4,128)(2,1)} copy(bf16[2,16,2,4,128]{4,3,2,1,0:T(4,128)(2,1)} %bitcast.7) | data formatting | bytes 131072
  37.5 0.0 copy-done
  37.5 0.5 %copy.11 = f32[16]{0:T(128)} copy(f32[16]{0:T(128)S(1)} %bitcast.11) | data formatting | bytes 128
Async XLA Ops:
  36.0 1.5 %copy-start = (f32[1,16]{1,0:T(1,128)S(1)}, f32[1,16]{1,0:T(1,128)}, u32[]{:S(2)}) copy-start(f32[1,16]{1,0:T(1,128)} %get-tuple-element.5) | copy-start | bytes 196

commit v2 on v1

--- a/solution.py
+++ b/solution.py
@@ -14,6 +14,9 @@
 FOURIER_POINTS = 4096
 DROPS = 32
 LANES = 128
+NX, NY = 4, 8
+ALONG_X = ((2, 0), (1, 0), (3, 0))
+ALONG_Y = ((0, 4), (0, 3), (0, 5), (0, 2), (0, 6), (0, 1), (0, 7))
 MESH = pl.DeviceIdType.MESH
 F32 = jnp.float32
 
@@ -58,26 +61,27 @@
     taps_hbm, lags_hbm, gain_hbm, symbols_hbm, noise_hbm, std_hbm,
     detected_ref, error_ref,
     taps_v, lags_v, gain_v, symbols_v, noise_v, std_v,
-    packed, padded, column, gathered, table, channel, noise_f, out_f, row_send, rows, sum_send, sums,
-    in_sems, send_sems, recv_sems,
+    packed, padded, column, gathered, table, channel, noise_f, out_f, out_v, row_send, rows, sum_send, sums,
+    in_sems, send_sems, recv_sems, ready,
 ):
     n_freq, n_drop = lax.axis_size("freq"), lax.axis_size("drop")
     freq, drop = lax.axis_index("freq"), lax.axis_index("drop")
     barrier = pltpu.get_barrier_semaphore()
 
-    def freq_peer(i):
-        return {"freq": lax.rem(freq + i, n_freq)}
-
-    def drop_peer(i):
-        return {"drop": lax.rem(drop + i, n_drop)}
-
-    @pl.loop(1, n_freq)
-    def _(i):
-        pl.semaphore_signal(barrier, inc=1, device_id=freq_peer(i), device_id_type=MESH)
-
-    @pl.loop(1, n_drop)
-    def _(i):
-        pl.semaphore_signal(barrier, inc=1, device_id=drop_peer(i), device_id_type=MESH)
+    x, y = freq // NY, lax.rem(freq, NY)
+
+    def peer(dx, dy):
+        return {"freq": lax.rem(x + dx, NX) * NY + lax.rem(y + dy, NY)}
+
+    def signal(semaphore, device):
+        pl.semaphore_signal(semaphore, inc=1, device_id=device, device_id_type=MESH)
+
+    for dx, dy in ALONG_Y + ALONG_X:
+        signal(barrier, peer(dx, dy))
+
+    @pl.loop(drop + 1, n_drop)
+    def _(i):
+        signal(barrier, {"drop": i})
 
     loads = [
         pltpu.make_async_copy(src, dst, in_sems.at[i])
@@ -101,17 +105,23 @@
     packed[...] = own
     gathered[freq] = own
 
-    pl.semaphore_wait(barrier, n_freq + n_drop - 2)
-
-    def send_taps(i):
+    pl.semaphore_wait(barrier, NX + NY - 2 + drop)
+
+    def copy_to(device, src, dst, i):
         return pltpu.make_async_remote_copy(
-            src_ref=packed, dst_ref=gathered.at[freq], send_sem=send_sems.at[0], recv_sem=recv_sems.at[0],
-            device_id=freq_peer(i), device_id_type=MESH,
+            src_ref=src, dst_ref=dst, send_sem=send_sems.at[i], recv_sem=recv_sems.at[i],
+            device_id=device, device_id_type=MESH,
         )
 
-    @pl.loop(1, n_freq)
-    def _(i):
-        send_taps(i).start()
+    def all_of(ref, n, i):
+        return copy_to(peer(0, 1), ref.at[pl.ds(0, n)], ref.at[pl.ds(0, n)], i)
+
+    for dx, dy in ALONG_Y:
+        copy_to(peer(dx, dy), packed, gathered.at[freq], 0).start()
+
+    @pl.loop(0, drop)
+    def _(i):
+        signal(ready, {"drop": i})
 
     loads[1].wait()
     loads[2].wait()
@@ -141,10 +151,11 @@
         at = pl.ds(pl.multiple_of(i * 64, 64), 64)
         noise_f[at, :] = noise_v[at, :].astype(F32)
 
-    pltpu.make_async_remote_copy(
-        src_ref=gathered.at[pl.ds(0, n_freq - 1)], dst_ref=gathered.at[pl.ds(0, n_freq - 1)],
-        send_sem=send_sems.at[0], recv_sem=recv_sems.at[0], device_id=freq_peer(1), device_id_type=MESH,
-    ).wait_recv()
+    all_of(gathered, NY - 1, 0).wait_recv()
+    mine = gathered.at[pl.ds(x * NY, NY)]
+    for dx, dy in ALONG_X:
+        copy_to(peer(dx, dy), mine, mine, 1).start()
+    all_of(gathered, (NX - 1) * NY, 1).wait_recv()
     response = jnp.dot(
         gathered[...].reshape(RX * TX, LANES), table[...],
         precision=lax.Precision.HIGHEST, preferred_element_type=F32,
@@ -210,15 +221,12 @@
     row_send[...] = row
     rows[freq] = row
 
-    def send_row(i):
-        return pltpu.make_async_remote_copy(
-            src_ref=row_send, dst_ref=rows.at[freq], send_sem=send_sems.at[1], recv_sem=recv_sems.at[1],
-            device_id=freq_peer(i), device_id_type=MESH,
-        )
-
-    @pl.loop(1, n_freq)
-    def _(i):
-        send_row(i).start()
+    @pl.loop(0, n_freq - 1)
+    def _(i):
+        far_x, far_y = lax.rem(i, NX), i // NX
+        dx = NX // 2 + (far_x + 1) // 2 * (2 * lax.rem(far_x, 2) - 1)
+        dy = NY // 2 + (far_y + 1) // 2 * (2 * lax.rem(far_y, 2) - 1)
+        copy_to(peer(dx, dy), row_send, rows.at[freq], 2).start()
 
     loads[3].wait()
     sent = []
@@ -232,14 +240,8 @@
                 )
             )
 
-    def all_rows(ref, n, i):
-        pltpu.make_async_remote_copy(
-            src_ref=ref.at[pl.ds(0, n - 1)], dst_ref=ref.at[pl.ds(0, n - 1)],
-            send_sem=send_sems.at[i], recv_sem=recv_sems.at[i], device_id=freq_peer(1), device_id_type=MESH,
-        ).wait_recv()
-        return jnp.sum(ref[...], axis=0)
-
-    row = all_rows(rows, n_freq, 1)
+    all_of(rows, n_freq - 1, 2).wait_recv()
+    row = jnp.sum(rows[...], axis=0)
     lane = lax.broadcasted_iota(jnp.int32, (1, LANES), 1)
     power = [
         jnp.sum(jnp.where(lane == 32 + d, row, 0.0), axis=1, keepdims=True) * (1.0 / (FOURIER_POINTS * RX * TX))
@@ -249,15 +251,17 @@
     sum_send[...] = weighted
     sums[drop] = weighted
 
-    def send_sum(i):
-        return pltpu.make_async_remote_copy(
-            src_ref=sum_send, dst_ref=sums.at[drop], send_sem=send_sems.at[2], recv_sem=recv_sems.at[2],
-            device_id=drop_peer(i), device_id_type=MESH,
-        )
-
-    @pl.loop(1, n_drop)
-    def _(i):
-        send_sum(i).start()
+    @pl.loop(0, drop)
+    def _(i):
+        copy_to({"drop": i}, sum_send, sums.at[drop], 3).start()
+
+    @pl.when(drop < n_drop - 1)
+    def _():
+        pl.semaphore_wait(ready, n_drop - 1 - drop)
+
+    @pl.loop(drop + 1, n_drop)
+    def _(i):
+        copy_to({"drop": i}, sum_send, sums.at[drop], 3).start()
 
     for d in range(2):
         amplitude = std[d] * jnp.sqrt(jnp.broadcast_to(power[d], (8, LANES)))
@@ -265,17 +269,20 @@
             for c in range(2):
                 estimate = sent[4 * d + t][c] + (amplitude * solved[d][t][c]).reshape(SNRS, LANES)
                 out_f[pl.ds(128 * d + 4 * c + t, SNRS, stride=8), :] = estimate
-    detected_ref[...] = out_f[...].astype(jnp.bfloat16)
-
-    total = all_rows(sums, n_drop, 2)
+    out_v[...] = out_f[...].astype(jnp.bfloat16)
+    store = pltpu.make_async_copy(out_v, detected_ref, in_sems.at[6])
+    store.start()
+
+    all_of(sums, n_drop - 1, 3).wait_recv()
+    total = jnp.sum(sums[...], axis=0)
     total = total[:, 0:SNRS] + total[:, SNRS : 2 * SNRS]
     error_ref[...] = RX * total / (DROPS * TX * FOURIER_POINTS)
 
-    for i, (ref, n) in enumerate(((gathered, n_freq), (rows, n_freq), (sums, n_drop))):
-        pltpu.make_async_remote_copy(
-            src_ref=ref.at[pl.ds(0, n - 1)], dst_ref=ref.at[pl.ds(0, n - 1)],
-            send_sem=send_sems.at[i], recv_sem=recv_sems.at[i], device_id=freq_peer(1), device_id_type=MESH,
-        ).wait_send()
+    store.wait()
+    all_of(gathered, NY - 1, 0).wait_send()
+    all_of(gathered, (NX - 1) * NY, 1).wait_send()
+    all_of(rows, n_freq - 1, 2).wait_send()
+    all_of(sums, n_drop - 1, 3).wait_send()
 
 
 def shards(taps, echo_lags, front_gain, symbols, noise, noise_std):
@@ -288,7 +295,7 @@
             jax.ShapeDtypeStruct((1, SNRS), F32),
         ),
         in_specs=[pl.BlockSpec(memory_space=pltpu.HBM)] * 6,
-        out_specs=(pl.BlockSpec(memory_space=pltpu.VMEM), pl.BlockSpec(memory_space=pltpu.VMEM)),
+        out_specs=(pl.BlockSpec(memory_space=pl.ANY), pl.BlockSpec(memory_space=pltpu.VMEM)),
         scratch_shapes=[
             vmem((2, 2, TX, TAPS), F32),
             vmem((2, TAPS), jnp.int32),
@@ -304,22 +311,29 @@
             vmem((4, RX * TX, LANES), F32),
             vmem((2 * SNRS * 2 * RX, LANES), F32),
             vmem((2 * SNRS * 8, LANES), F32),
+            vmem((2 * SNRS * 8, LANES), jnp.bfloat16),
             vmem((1, LANES), F32),
             vmem((n_freq, 1, LANES), F32),
             vmem((1, LANES), F32),
             vmem((n_drop, 1, LANES), F32),
-            pltpu.SemaphoreType.DMA((6,)),
-            pltpu.SemaphoreType.DMA((3,)),
-            pltpu.SemaphoreType.DMA((3,)),
+            pltpu.SemaphoreType.DMA((7,)),
+            pltpu.SemaphoreType.DMA((4,)),
+            pltpu.SemaphoreType.DMA((4,)),
+            pltpu.SemaphoreType.REGULAR,
         ],
-        compiler_params=pltpu.CompilerParams(collective_id=0, has_side_effects=True),
+        compiler_params=pltpu.CompilerParams(collective_id=0, has_side_effects=True, vmem_limit_bytes=16 << 20),
     )(
-        jnp.transpose(taps, (0, 1, 3, 2)),
-        echo_lags,
-        front_gain.reshape(1, LANES),
-        symbols.reshape(2 * SNRS * TX, LANES),
-        noise.reshape(2 * SNRS * 2 * RX, LANES),
-        noise_std,
+        *[
+            pltpu.with_memory_space_constraint(v, pltpu.HBM)
+            for v in (
+                jnp.transpose(taps, (0, 1, 3, 2)),
+                echo_lags,
+                front_gain.reshape(1, LANES),
+                symbols.reshape(2 * SNRS * TX, LANES),
+                noise.reshape(2 * SNRS * 2 * RX, LANES),
+                noise_std,
+            )
+        ]
     )
     return detected.reshape(2, SNRS, 2, TX, LANES), error.reshape(SNRS)
 

time: 38.2 us -> 36.7 us (0.961)
  local copies, waits for them, and re-layouts: 2.01 us -> 1.14 us
  Pallas kernels: 35.3 us -> 34.7 us
    unnamed x4 -> x2, local copies, waits for them, and re-layouts: 2.01 us -> 1.14 us
    pallas_call x1, Pallas kernels: 35.3 us -> 34.7 us  [shards(): pl.pallas_call(kernel, out_shape=(jax.ShapeDtypeStruct((2 * SNRS * 8, LAN...]
where the time goes in v2:
time: 36.7 us; the launch traced here: 36.5 us
  Pallas kernels  34.7 us (95%)
  local copies, waits for them, and re-layouts  1.14 us (3%)
  between operations  0.64 us (2%)
    pallas_call x1, Pallas kernels, shards(): pl.pallas_call(kernel, out_shape=(jax.ShapeDtypeStruct((2 * SNRS * 8, LAN...  34.7 us
    unnamed x2, local copies, waits for them, and re-layouts  1.14 us

profile of v2, /device:TPU:1, one launch (start us, length us, event | category | flops | bytes accessed | tf_op | source)
XLA Modules:
  0.0 36.5 jit_solution(825985275130980368)
XLA Ops:
  0.6 34.7 %shard_map.77 = (bf16[256,128]{1,0:T(8,128)(2,1)S(1)}, f32[1,16]{1,0:T(1,128)S(1)}) custom-call(f32[2,2,4,23]{3,2,1,0:T(4,128)} %bitcast.10, s32[2,23]{1,0:T(2,128)} %lags_hbm.1, f32[1,128]{1,0:T(1,128)} %bitcast.11, s32[128,128]{1,0:T(8,128)} %bitcast.9, bf16[2048,128]{1,0:T(8,128)(2,1)} %bitcast.8, f32[2,16]{1,0:T(2,128)} %std_hbm.1), custom_call_target="tpu_custom_call" | custom-call | tf_op jit(solution)/shard_map/pallas_call | solution.py:291
  35.4 0.6 %copy.10 = bf16[2,16,2,4,128]{4,3,2,1,0:T(4,128)(2,1)} copy(bf16[2,16,2,4,128]{4,3,2,1,0:T(4,128)(2,1)S(1)} %bitcast.6) | data formatting | bytes 131072
  36.0 0.5 %copy.11 = f32[16]{0:T(128)} copy(f32[16]{0:T(128)S(1)} %bitcast.7) | data formatting | bytes 128

commit v3 on v2

--- a/solution.py
+++ b/solution.py
@@ -16,7 +16,6 @@
 LANES = 128
 NX, NY = 4, 8
 ALONG_X = ((2, 0), (1, 0), (3, 0))
-ALONG_Y = ((0, 4), (0, 3), (0, 5), (0, 2), (0, 6), (0, 1), (0, 7))
 MESH = pl.DeviceIdType.MESH
 F32 = jnp.float32
 
@@ -62,7 +61,7 @@
     detected_ref, error_ref,
     taps_v, lags_v, gain_v, symbols_v, noise_v, std_v,
     packed, padded, column, gathered, table, channel, noise_f, out_f, out_v, row_send, rows, sum_send, sums,
-    in_sems, send_sems, recv_sems, ready,
+    in_sems, send_sems, recv_sems, y_ready, ready,
 ):
     n_freq, n_drop = lax.axis_size("freq"), lax.axis_size("drop")
     freq, drop = lax.axis_index("freq"), lax.axis_index("drop")
@@ -75,13 +74,6 @@
 
     def signal(semaphore, device):
         pl.semaphore_signal(semaphore, inc=1, device_id=device, device_id_type=MESH)
-
-    for dx, dy in ALONG_Y + ALONG_X:
-        signal(barrier, peer(dx, dy))
-
-    @pl.loop(drop + 1, n_drop)
-    def _(i):
-        signal(barrier, {"drop": i})
 
     loads = [
         pltpu.make_async_copy(src, dst, in_sems.at[i])
@@ -95,6 +87,24 @@
     for load in loads:
         load.start()
 
+    upper = y // 5
+    order = (1 - upper) * (2 * y - 1 + (NY - y) // NY) + upper * 2 * (NY - y)
+
+    def y_peer(i):
+        odd = lax.rem(i, 2)
+        return {"freq": x * NY + odd * ((i + 1) // 2) + (1 - odd) * lax.rem(NY - i // 2, NY)}
+
+    for dx, dy in ALONG_X:
+        signal(barrier, peer(dx, dy))
+
+    @pl.loop(order + 1, NY)
+    def _(i):
+        signal(barrier, y_peer(i))
+
+    @pl.loop(drop + 1, n_drop)
+    def _(i):
+        signal(barrier, {"drop": i})
+
     padded[...] = jnp.zeros_like(padded)
     loads[0].wait()
     for q in range(4):
@@ -103,9 +113,9 @@
     for q in range(1, 4):
         own = own + pltpu.roll(padded[q], 32 * q, 1)
     packed[...] = own
-    gathered[freq] = own
-
-    pl.semaphore_wait(barrier, NX + NY - 2 + drop)
+    gathered[y, x] = own
+
+    pl.semaphore_wait(barrier, NX - 1 + order + drop)
 
     def copy_to(device, src, dst, i):
         return pltpu.make_async_remote_copy(
@@ -116,8 +126,12 @@
     def all_of(ref, n, i):
         return copy_to(peer(0, 1), ref.at[pl.ds(0, n)], ref.at[pl.ds(0, n)], i)
 
-    for dx, dy in ALONG_Y:
-        copy_to(peer(dx, dy), packed, gathered.at[freq], 0).start()
+    for dx, dy in ALONG_X:
+        copy_to(peer(dx, dy), packed, gathered.at[y, x], 0).start()
+
+    @pl.loop(0, order)
+    def _(i):
+        signal(y_ready, y_peer(i))
 
     @pl.loop(0, drop)
     def _(i):
@@ -151,11 +165,21 @@
         at = pl.ds(pl.multiple_of(i * 64, 64), 64)
         noise_f[at, :] = noise_v[at, :].astype(F32)
 
-    all_of(gathered, NY - 1, 0).wait_recv()
-    mine = gathered.at[pl.ds(x * NY, NY)]
-    for dx, dy in ALONG_X:
-        copy_to(peer(dx, dy), mine, mine, 1).start()
-    all_of(gathered, (NX - 1) * NY, 1).wait_recv()
+    all_of(gathered.at[0], NX - 1, 0).wait_recv()
+
+    @pl.loop(0, order)
+    def _(i):
+        copy_to(y_peer(i), gathered.at[y], gathered.at[y], 1).start()
+
+    @pl.when(order < NY - 1)
+    def _():
+        pl.semaphore_wait(y_ready, NY - 1 - order)
+
+    @pl.loop(0, NY - 1 - order)
+    def _(i):
+        copy_to(y_peer(NY - 1 - i), gathered.at[y], gathered.at[y], 1).start()
+
+    all_of(gathered, NY - 1, 1).wait_recv()
     response = jnp.dot(
         gathered[...].reshape(RX * TX, LANES), table[...],
         precision=lax.Precision.HIGHEST, preferred_element_type=F32,
@@ -163,12 +187,13 @@
     for q in range(4):
         channel[q] = response[:, LANES * q : LANES * (q + 1)]
 
-    def match_step(r, so_far):
+    def match_step(i, so_far):
+        r = lax.rem(i, NX) * NY + i // NX
         result = []
         for d in range(2):
             noise = [noise_f[pl.ds(1024 * d + 32 * c + r, SNRS, stride=64), :].reshape(2, 8, LANES) for c in range(2)]
             for t in range(TX):
-                h = [channel[2 * d + c, pl.ds(TX * r + t, 1), :] for c in range(2)]
+                h = [channel[2 * d + c, pl.ds(TX * i + t, 1), :] for c in range(2)]
                 h = [jnp.broadcast_to(v, (8, LANES))[None] for v in h]
                 re, im = cmul_conj(h, noise)
                 old_re, old_im = so_far[4 * d + t]
@@ -279,8 +304,8 @@
     error_ref[...] = RX * total / (DROPS * TX * FOURIER_POINTS)
 
     store.wait()
-    all_of(gathered, NY - 1, 0).wait_send()
-    all_of(gathered, (NX - 1) * NY, 1).wait_send()
+    all_of(gathered.at[0], NX - 1, 0).wait_send()
+    all_of(gathered, NY - 1, 1).wait_send()
     all_of(rows, n_freq - 1, 2).wait_send()
     all_of(sums, n_drop - 1, 3).wait_send()
 
@@ -306,7 +331,7 @@
             vmem((TX, LANES), F32),
             vmem((4, TX, LANES), F32),
             vmem((LANES, LANES), F32),
-            vmem((n_freq, TX, LANES), F32),
+            vmem((NY, NX, TX, LANES), F32),
             vmem((LANES, 4 * LANES), F32),
             vmem((4, RX * TX, LANES), F32),
             vmem((2 * SNRS * 2 * RX, LANES), F32),
@@ -319,6 +344,7 @@
             pltpu.SemaphoreType.DMA((7,)),
             pltpu.SemaphoreType.DMA((4,)),
             pltpu.SemaphoreType.DMA((4,)),
+            pltpu.SemaphoreType.REGULAR,
             pltpu.SemaphoreType.REGULAR,
         ],
         compiler_params=pltpu.CompilerParams(collective_id=0, has_side_effects=True, vmem_limit_bytes=16 << 20),

time: 36.7 us -> 35.3 us (0.962)
  Pallas kernels: 34.7 us -> 33.4 us
    pallas_call x1, Pallas kernels: 34.7 us -> 33.4 us  [shards(): pl.pallas_call(kernel, out_shape=(jax.ShapeDtypeStruct((2 * SNRS * 8, LAN...]
where the time goes in v3:
time: 35.3 us; the launch traced here: 35.2 us
  Pallas kernels  33.4 us (95%)
  local copies, waits for them, and re-layouts  1.14 us (3%)
  between operations  0.64 us (2%)
    pallas_call x1, Pallas kernels, shards(): pl.pallas_call(kernel, out_shape=(jax.ShapeDtypeStruct((2 * SNRS * 8, LAN...  33.4 us
    unnamed x2, local copies, waits for them, and re-layouts  1.14 us

profile of v3, /device:TPU:1, one launch (start us, length us, event | category | flops | bytes accessed | tf_op | source)
XLA Modules:
  0.0 35.2 jit_solution(1430572444708233660)
XLA Ops:
  0.6 33.4 %shard_map.77 = (bf16[256,128]{1,0:T(8,128)(2,1)S(1)}, f32[1,16]{1,0:T(1,128)S(1)}) custom-call(f32[2,2,4,23]{3,2,1,0:T(4,128)} %bitcast.10, s32[2,23]{1,0:T(2,128)} %lags_hbm.1, f32[1,128]{1,0:T(1,128)} %bitcast.11, s32[128,128]{1,0:T(8,128)} %bitcast.9, bf16[2048,128]{1,0:T(8,128)(2,1)} %bitcast.8, f32[2,16]{1,0:T(2,128)} %std_hbm.1), custom_call_target="tpu_custom_call" | custom-call | tf_op jit(solution)/shard_map/pallas_call | solution.py:316
  34.0 0.6 %copy.10 = bf16[2,16,2,4,128]{4,3,2,1,0:T(4,128)(2,1)} copy(bf16[2,16,2,4,128]{4,3,2,1,0:T(4,128)(2,1)S(1)} %bitcast.6) | data formatting | bytes 131072
  34.7 0.5 %copy.11 = f32[16]{0:T(128)} copy(f32[16]{0:T(128)S(1)} %bitcast.7) | data formatting | bytes 128

commit v4 on v3

--- a/solution.py
+++ b/solution.py
@@ -15,6 +15,7 @@
 DROPS = 32
 LANES = 128
 NX, NY = 4, 8
+NEAR = 6
 ALONG_X = ((2, 0), (1, 0), (3, 0))
 MESH = pl.DeviceIdType.MESH
 F32 = jnp.float32
@@ -38,7 +39,6 @@
 
 
 def over_sublanes(x):
-    x = (x[0:8] + x[8:16]) + (x[16:24] + x[24:32])
     x = x + pltpu.roll(x, 4, 0)
     x = x + pltpu.roll(x, 2, 0)
     return x + pltpu.roll(x, 1, 0)
@@ -50,6 +50,15 @@
 
 def cmul_conj(a, b):
     return a[0] * b[0] + a[1] * b[1], a[0] * b[1] - a[1] * b[0]
+
+
+def cadd(a, b):
+    return a[0] + b[0], a[1] + b[1]
+
+
+def halves(x):
+    high = x.astype(jnp.bfloat16)
+    return high, (x - high.astype(F32)).astype(jnp.bfloat16)
 
 
 def csub(a, b):
@@ -90,9 +99,12 @@
     upper = y // 5
     order = (1 - upper) * (2 * y - 1 + (NY - y) // NY) + upper * 2 * (NY - y)
 
+    def y_at(i):
+        odd = lax.rem(i, 2)
+        return odd * ((i + 1) // 2) + (1 - odd) * lax.rem(NY - i // 2, NY)
+
     def y_peer(i):
-        odd = lax.rem(i, 2)
-        return {"freq": x * NY + odd * ((i + 1) // 2) + (1 - odd) * lax.rem(NY - i // 2, NY)}
+        return {"freq": x * NY + y_at(i)}
 
     for dx, dy in ALONG_X:
         signal(barrier, peer(dx, dy))
@@ -117,21 +129,21 @@
 
     pl.semaphore_wait(barrier, NX - 1 + order + drop)
 
-    def copy_to(device, src, dst, i):
+    def copy_to(device, src, dst, i, received=None):
         return pltpu.make_async_remote_copy(
-            src_ref=src, dst_ref=dst, send_sem=send_sems.at[i], recv_sem=recv_sems.at[i],
+            src_ref=src, dst_ref=dst, send_sem=send_sems.at[i], recv_sem=recv_sems.at[i if received is None else received],
             device_id=device, device_id_type=MESH,
         )
 
-    def all_of(ref, n, i):
-        return copy_to(peer(0, 1), ref.at[pl.ds(0, n)], ref.at[pl.ds(0, n)], i)
+    def all_of(ref, n, i, received=None):
+        return copy_to(peer(0, 1), ref.at[pl.ds(0, n)], ref.at[pl.ds(0, n)], i, received)
 
     for dx, dy in ALONG_X:
         copy_to(peer(dx, dy), packed, gathered.at[y, x], 0).start()
 
     @pl.loop(0, order)
     def _(i):
-        signal(y_ready, y_peer(i))
+        signal(y_ready.at[order], y_peer(i))
 
     @pl.loop(0, drop)
     def _(i):
@@ -152,10 +164,13 @@
         cosine, sine = cos_sin((lag * tone) & (FOURIER_POINTS - 1))
         cosine = cosine * gain
         sine = sine * gain
-        table[64 * d : 64 * d + 32, 256 * d : 256 * d + 128] = cosine
-        table[64 * d + 32 : 64 * d + 64, 256 * d : 256 * d + 128] = sine
-        table[64 * d : 64 * d + 32, 256 * d + 128 : 256 * d + 256] = -sine
-        table[64 * d + 32 : 64 * d + 64, 256 * d + 128 : 256 * d + 256] = cosine
+        for at, block in ((0, (cosine, -sine)), (32, (sine, cosine))):
+            for c in range(2):
+                high, low = halves(block[c])
+                lanes = slice(LANES * c, LANES * (c + 1))
+                table[d, at : at + 32, lanes] = high
+                table[d, at + 64 : at + 96, lanes] = high
+                table[d, at + 128 + 64 * d : at + 160 + 64 * d, lanes] = low
     std = [jnp.broadcast_to(turned[0:SNRS, 2 + d : 3 + d], (SNRS, LANES)).reshape(2, 8, LANES) for d in range(2)]
 
     loads[4].wait()
@@ -167,28 +182,47 @@
 
     all_of(gathered.at[0], NX - 1, 0).wait_recv()
 
+    def send_row_of_taps(i):
+        late = lax.rem(y - y_at(i) + NY + 2, NY) // NEAR
+        copy_to(y_peer(i), gathered.at[y], gathered.at[y], 1, 1 + 3 * late).start()
+
     @pl.loop(0, order)
     def _(i):
-        copy_to(y_peer(i), gathered.at[y], gathered.at[y], 1).start()
-
-    @pl.when(order < NY - 1)
-    def _():
-        pl.semaphore_wait(y_ready, NY - 1 - order)
-
-    @pl.loop(0, NY - 1 - order)
-    def _(i):
-        copy_to(y_peer(NY - 1 - i), gathered.at[y], gathered.at[y], 1).start()
-
-    all_of(gathered, NY - 1, 1).wait_recv()
-    response = jnp.dot(
-        gathered[...].reshape(RX * TX, LANES), table[...],
-        precision=lax.Precision.HIGHEST, preferred_element_type=F32,
-    )
-    for q in range(4):
-        channel[q] = response[:, LANES * q : LANES * (q + 1)]
-
+        send_row_of_taps(i)
+
+    @pl.loop(order + 1, NY)
+    def _(i):
+        pl.semaphore_wait(y_ready.at[i], 1)
+        send_row_of_taps(i)
+
+    def respond(places):
+        rows_of = [gathered[lax.rem(y + 6 + i, NY)].reshape(NX * TX, LANES) for i in places]
+        full = jnp.concatenate(rows_of, axis=0)
+        high = full.astype(jnp.bfloat16).astype(F32)
+        low = pltpu.roll(full - high, 64, 1)
+        first = lax.broadcasted_iota(jnp.int32, full.shape, 1) < 64
+        at = slice(NX * TX * places[0], NX * TX * (places[-1] + 1))
+        for d in range(2):
+            mixed = jnp.where(first, high, low) if d == 0 else jnp.where(first, low, high)
+            left = jnp.concatenate([mixed, high], axis=1).astype(jnp.bfloat16)
+            response = jnp.dot(left, table[d], preferred_element_type=F32)
+            for c in range(2):
+                channel[2 * d + c, at, :] = response[:, LANES * c : LANES * (c + 1)]
+
+    def gram_terms(groups):
+        result = []
+        for d in range(2):
+            diagonal, upper = [0.0] * TX, {}
+            for g in groups:
+                h = [[channel[2 * d + c, pl.ds(32 * g + t, 8, stride=TX), :] for c in range(2)] for t in range(TX)]
+                for t in range(TX):
+                    diagonal[t] = diagonal[t] + h[t][0] * h[t][0] + h[t][1] * h[t][1]
+                    for u in range(t + 1, TX):
+                        upper[t, u] = cadd(upper.get((t, u), (0.0, 0.0)), cmul_conj(h[t], h[u]))
+            result.append((diagonal, upper))
+        return result
     def match_step(i, so_far):
-        r = lax.rem(i, NX) * NY + i // NX
+        r = lax.rem(i, NX) * NY + lax.rem(y + 6 + i // NX, NY)
         result = []
         for d in range(2):
             noise = [noise_f[pl.ds(1024 * d + 32 * c + r, SNRS, stride=64), :].reshape(2, 8, LANES) for c in range(2)]
@@ -201,17 +235,20 @@
         return tuple(result)
 
     nothing = jnp.zeros((2, 8, LANES), F32)
-    match = lax.fori_loop(0, RX, match_step, ((nothing, nothing),) * 8, unroll=4)
+    all_of(gathered, NEAR - 1, 1).wait_recv()
+    respond(range(NEAR))
+    early = gram_terms(range(NEAR // 2))
+    match = lax.fori_loop(0, NX * NEAR, match_step, ((nothing, nothing),) * 8, unroll=4)
+
+    all_of(gathered, NY - NEAR, 1, 4).wait_recv()
+    respond(range(NEAR, NY))
+    late = gram_terms(range(NEAR // 2, NY // 2))
+    match = lax.fori_loop(NX * NEAR, RX, match_step, match, unroll=True)
 
     solved, totals, powers = [], [], []
     for d in range(2):
-        h = [[channel[2 * d + c, pl.ds(t, RX, stride=TX), :] for c in range(2)] for t in range(TX)]
-        diagonal = [over_sublanes(h[t][0] * h[t][0] + h[t][1] * h[t][1]) for t in range(TX)]
-        upper = {}
-        for t in range(TX):
-            for u in range(t + 1, TX):
-                re, im = cmul_conj(h[t], h[u])
-                upper[t, u] = over_sublanes(re), over_sublanes(im)
+        diagonal = [over_sublanes(early[d][0][t] + late[d][0][t]) for t in range(TX)]
+        upper = {at: tuple(over_sublanes(v) for v in cadd(early[d][1][at], late[d][1][at])) for at in early[d][1]}
         powers.append((diagonal[0] + diagonal[1]) + (diagonal[2] + diagonal[3]))
         right = [match[4 * d + t] for t in range(TX)]
         inverse = []
@@ -310,6 +347,17 @@
     all_of(sums, n_drop - 1, 3).wait_send()
 
 
+def write_out(detected_ref, error_ref, detected_out, error_out, sems):
+    copies = [
+        pltpu.make_async_copy(src, dst, sems.at[i])
+        for i, (src, dst) in enumerate(((detected_ref, detected_out), (error_ref, error_out)))
+    ]
+    for copy in copies:
+        copy.start()
+    for copy in copies:
+        copy.wait()
+
+
 def shards(taps, echo_lags, front_gain, symbols, noise, noise_std):
     n_freq, n_drop = lax.axis_size("freq"), lax.axis_size("drop")
     vmem = pltpu.VMEM
@@ -332,7 +380,7 @@
             vmem((4, TX, LANES), F32),
             vmem((LANES, LANES), F32),
             vmem((NY, NX, TX, LANES), F32),
-            vmem((LANES, 4 * LANES), F32),
+            vmem((2, 2 * LANES, 2 * LANES), jnp.bfloat16),
             vmem((4, RX * TX, LANES), F32),
             vmem((2 * SNRS * 2 * RX, LANES), F32),
             vmem((2 * SNRS * 8, LANES), F32),
@@ -343,8 +391,8 @@
             vmem((n_drop, 1, LANES), F32),
             pltpu.SemaphoreType.DMA((7,)),
             pltpu.SemaphoreType.DMA((4,)),
-            pltpu.SemaphoreType.DMA((4,)),
-            pltpu.SemaphoreType.REGULAR,
+            pltpu.SemaphoreType.DMA((5,)),
+            pltpu.SemaphoreType.REGULAR((NY,)),
             pltpu.SemaphoreType.REGULAR,
         ],
         compiler_params=pltpu.CompilerParams(collective_id=0, has_side_effects=True, vmem_limit_bytes=16 << 20),
@@ -361,6 +409,17 @@
             )
         ]
     )
+    detected, error = pl.pallas_call(
+        write_out,
+        out_shape=(
+            jax.ShapeDtypeStruct((2 * SNRS * 8, LANES), jnp.bfloat16),
+            jax.ShapeDtypeStruct((1, SNRS), F32),
+        ),
+        in_specs=[pl.BlockSpec(memory_space=pltpu.VMEM)] * 2,
+        out_specs=[pl.BlockSpec(memory_space=pltpu.HBM)] * 2,
+        scratch_shapes=[pltpu.SemaphoreType.DMA((2,))],
+        compiler_params=pltpu.CompilerParams(vmem_limit_bytes=1 << 20),
+    )(detected, error)
     return detected.reshape(2, SNRS, 2, TX, LANES), error.reshape(SNRS)
 
 

time: 35.3 us -> 34.8 us (0.986)
  local copies, waits for them, and re-layouts: 1.14 us -> 0 us
  Pallas kernels: 33.4 us -> 34 us
    unnamed x2 -> x0, local copies, waits for them, and re-layouts: 1.14 us -> none
    pallas_call x0 -> x1, Pallas kernels: none -> 0.65 us  [shards(): pl.pallas_call(write_out, out_shape=(jax.ShapeDtypeStruct((2 * SNRS * 8,...]
where the time goes in v4:
time: 34.8 us; the launch traced here: 34.6 us
  Pallas kernels  34 us (98%)
  between operations  0.64 us (2%)
    pallas_call x1, Pallas kernels, shards(): pl.pallas_call(kernel, out_shape=(jax.ShapeDtypeStruct((2 * SNRS * 8, LAN...  33.3 us

profile of v4, /device:TPU:1, one launch (start us, length us, event | category | flops | bytes accessed | tf_op | source)
XLA Modules:
  0.0 34.6 jit_solution(6964237004695288337)
XLA Ops:
  0.6 33.3 %shard_map.77 = (bf16[256,128]{1,0:T(8,128)(2,1)S(1)}, f32[1,16]{1,0:T(1,128)S(1)}) custom-call(f32[2,2,4,23]{3,2,1,0:T(4,128)} %bitcast.8, s32[2,23]{1,0:T(2,128)} %lags_hbm.1, f32[1,128]{1,0:T(1,128)} %bitcast.9, s32[128,128]{1,0:T(8,128)} %bitcast.7, bf16[2048,128]{1,0:T(8,128)(2,1)} %bitcast.6, f32[2,16]{1,0:T(2,128)} %std_hbm.1), custom_call_target="tpu_custom_call" | custom-call | tf_op jit(solution)/shard_map/pallas_call | solution.py:364
  34.0 0.7 %shard_map.78 = (bf16[256,128]{1,0:T(8,128)(2,1)}, f32[1,16]{1,0:T(1,128)}) custom-call(bf16[256,128]{1,0:T(8,128)(2,1)S(1)} %get-tuple-element.6.detected_ref, f32[1,16]{1,0:T(1,128)S(1)} %get-tuple-element.7.error_ref), custom_call_target="tpu_custom_call" | custom-call | tf_op jit(solution)/shard_map/pallas_call | solution.py:412

commit v5 on v4

--- a/solution.py
+++ b/solution.py
@@ -15,7 +15,7 @@
 DROPS = 32
 LANES = 128
 NX, NY = 4, 8
-NEAR = 6
+NEAR = 4
 ALONG_X = ((2, 0), (1, 0), (3, 0))
 MESH = pl.DeviceIdType.MESH
 F32 = jnp.float32
@@ -69,7 +69,7 @@
     taps_hbm, lags_hbm, gain_hbm, symbols_hbm, noise_hbm, std_hbm,
     detected_ref, error_ref,
     taps_v, lags_v, gain_v, symbols_v, noise_v, std_v,
-    packed, padded, column, gathered, table, channel, noise_f, out_f, out_v, row_send, rows, sum_send, sums,
+    packed, padded, column, gathered, table, channel, noise_f, noise_t, out_f, out_v, row_send, rows, sum_send, sums,
     in_sems, send_sems, recv_sems, y_ready, ready,
 ):
     n_freq, n_drop = lax.axis_size("freq"), lax.axis_size("drop")
@@ -117,6 +117,12 @@
     def _(i):
         signal(barrier, {"drop": i})
 
+    pl.semaphore_wait(barrier, NX - 1 + order + drop)
+
+    @pl.loop(0, order)
+    def _(i):
+        signal(y_ready.at[order], y_peer(i))
+
     padded[...] = jnp.zeros_like(padded)
     loads[0].wait()
     for q in range(4):
@@ -127,8 +133,6 @@
     packed[...] = own
     gathered[y, x] = own
 
-    pl.semaphore_wait(barrier, NX - 1 + order + drop)
-
     def copy_to(device, src, dst, i, received=None):
         return pltpu.make_async_remote_copy(
             src_ref=src, dst_ref=dst, send_sem=send_sems.at[i], recv_sem=recv_sems.at[i if received is None else received],
@@ -141,13 +145,10 @@
     for dx, dy in ALONG_X:
         copy_to(peer(dx, dy), packed, gathered.at[y, x], 0).start()
 
-    @pl.loop(0, order)
-    def _(i):
-        signal(y_ready.at[order], y_peer(i))
-
     @pl.loop(0, drop)
     def _(i):
         signal(ready, {"drop": i})
+
 
     loads[1].wait()
     loads[2].wait()
@@ -180,6 +181,12 @@
         at = pl.ds(pl.multiple_of(i * 64, 64), 64)
         noise_f[at, :] = noise_v[at, :].astype(F32)
 
+    @pl.loop(0, RX)
+    def _(r):
+        for q in range(4):
+            levels = noise_f[pl.ds(1024 * (q // 2) + 32 * (q % 2) + r, SNRS, stride=2 * RX), :]
+            noise_t[pl.ds(pl.multiple_of(SNRS * (RX * q + r), SNRS), SNRS), :] = levels
+
     all_of(gathered.at[0], NX - 1, 0).wait_recv()
 
     def send_row_of_taps(i):
@@ -221,29 +228,36 @@
                         upper[t, u] = cadd(upper.get((t, u), (0.0, 0.0)), cmul_conj(h[t], h[u]))
             result.append((diagonal, upper))
         return result
-    def match_step(i, so_far):
-        r = lax.rem(i, NX) * NY + lax.rem(y + 6 + i // NX, NY)
+    def matches(first, last, so_far, unroll):
         result = []
         for d in range(2):
-            noise = [noise_f[pl.ds(1024 * d + 32 * c + r, SNRS, stride=64), :].reshape(2, 8, LANES) for c in range(2)]
-            for t in range(TX):
-                h = [channel[2 * d + c, pl.ds(TX * i + t, 1), :] for c in range(2)]
-                h = [jnp.broadcast_to(v, (8, LANES))[None] for v in h]
-                re, im = cmul_conj(h, noise)
-                old_re, old_im = so_far[4 * d + t]
-                result.append((old_re + re, old_im + im))
-        return tuple(result)
+
+            def step(i, old, d=d):
+                r = lax.rem(i, NX) * NY + lax.rem(y + 6 + i // NX, NY)
+                noise = [
+                    noise_t[pl.ds(pl.multiple_of(SNRS * (RX * (2 * d + c) + r), SNRS), SNRS), :].reshape(2, 8, LANES)
+                    for c in range(2)
+                ]
+                new = []
+                for t in range(TX):
+                    h = [channel[2 * d + c, pl.ds(TX * i + t, 1), :] for c in range(2)]
+                    h = [jnp.broadcast_to(v, (8, LANES))[None] for v in h]
+                    new.append(cadd(old[t], cmul_conj(h, noise)))
+                return tuple(new)
+
+            result.extend(lax.fori_loop(first, last, step, tuple(so_far[TX * d : TX * (d + 1)]), unroll=unroll))
+        return result
 
     nothing = jnp.zeros((2, 8, LANES), F32)
     all_of(gathered, NEAR - 1, 1).wait_recv()
     respond(range(NEAR))
     early = gram_terms(range(NEAR // 2))
-    match = lax.fori_loop(0, NX * NEAR, match_step, ((nothing, nothing),) * 8, unroll=4)
+    match = matches(0, NX * NEAR, [(nothing, nothing)] * 8, 8)
 
     all_of(gathered, NY - NEAR, 1, 4).wait_recv()
     respond(range(NEAR, NY))
     late = gram_terms(range(NEAR // 2, NY // 2))
-    match = lax.fori_loop(NX * NEAR, RX, match_step, match, unroll=True)
+    match = matches(NX * NEAR, RX, match, True)
 
     solved, totals, powers = [], [], []
     for d in range(2):
@@ -382,6 +396,7 @@
             vmem((NY, NX, TX, LANES), F32),
             vmem((2, 2 * LANES, 2 * LANES), jnp.bfloat16),
             vmem((4, RX * TX, LANES), F32),
+            vmem((2 * SNRS * 2 * RX, LANES), F32),
             vmem((2 * SNRS * 2 * RX, LANES), F32),
             vmem((2 * SNRS * 8, LANES), F32),
             vmem((2 * SNRS * 8, LANES), jnp.bfloat16),

time: 34.8 us -> 33.9 us (0.974)
  Pallas kernels: 34 us -> 33.1 us
    pallas_call x1, Pallas kernels: 33.3 us -> 32.5 us  [shards(): pl.pallas_call(kernel, out_shape=(jax.ShapeDtypeStruct((2 * SNRS * 8, LAN...]
where the time goes in v5:
time: 33.9 us; the launch traced here: 33.8 us
  Pallas kernels  33.1 us (98%)
  between operations  0.64 us (2%)
    pallas_call x1, Pallas kernels, shards(): pl.pallas_call(kernel, out_shape=(jax.ShapeDtypeStruct((2 * SNRS * 8, LAN...  32.5 us

profile of v5, /device:TPU:1, one launch (start us, length us, event | category | flops | bytes accessed | tf_op | source)
XLA Modules:
  0.0 33.8 jit_solution(15783558601312249024)
XLA Ops:
  0.6 32.5 %shard_map.77 = (bf16[256,128]{1,0:T(8,128)(2,1)S(1)}, f32[1,16]{1,0:T(1,128)S(1)}) custom-call(f32[2,2,4,23]{3,2,1,0:T(4,128)} %bitcast.8, s32[2,23]{1,0:T(2,128)} %lags_hbm.1, f32[1,128]{1,0:T(1,128)} %bitcast.9, s32[128,128]{1,0:T(8,128)} %bitcast.7, bf16[2048,128]{1,0:T(8,128)(2,1)} %bitcast.6, f32[2,16]{1,0:T(2,128)} %std_hbm.1), custom_call_target="tpu_custom_call" | custom-call | tf_op jit(solution)/shard_map/pallas_call | solution.py:378
  33.1 0.7 %shard_map.78 = (bf16[256,128]{1,0:T(8,128)(2,1)}, f32[1,16]{1,0:T(1,128)}) custom-call(bf16[256,128]{1,0:T(8,128)(2,1)S(1)} %get-tuple-element.6.detected_ref, f32[1,16]{1,0:T(1,128)S(1)} %get-tuple-element.7.error_ref), custom_call_target="tpu_custom_call" | custom-call | tf_op jit(solution)/shard_map/pallas_call | solution.py:427

commit v6 on v5

--- a/solution.py
+++ b/solution.py
@@ -121,7 +121,7 @@
 
     @pl.loop(0, order)
     def _(i):
-        signal(y_ready.at[order], y_peer(i))
+        signal(y_ready, y_peer(i))
 
     padded[...] = jnp.zeros_like(padded)
     loads[0].wait()
@@ -197,10 +197,13 @@
     def _(i):
         send_row_of_taps(i)
 
-    @pl.loop(order + 1, NY)
-    def _(i):
-        pl.semaphore_wait(y_ready.at[i], 1)
-        send_row_of_taps(i)
+    @pl.when(order < NY - 1)
+    def _():
+        pl.semaphore_wait(y_ready, NY - 1 - order)
+
+    @pl.loop(0, NY - 1 - order)
+    def _(i):
+        send_row_of_taps(NY - 1 - i)
 
     def respond(places):
         rows_of = [gathered[lax.rem(y + 6 + i, NY)].reshape(NX * TX, LANES) for i in places]
@@ -288,12 +291,13 @@
 
     lane8 = lax.broadcasted_iota(jnp.int32, (8, LANES), 1)
     sub8 = lax.broadcasted_iota(jnp.int32, (8, LANES), 0)
-    power_rows = jnp.where(sub8 == 0, powers[0], jnp.where(sub8 == 1, powers[1], 0.0))
-    stacked = [totals[0][0], totals[0][1], totals[1][0], totals[1][1], power_rows]
+    stacked = [totals[0][0], totals[0][1], totals[1][0], totals[1][1]]
     row = jnp.zeros((8, LANES), F32)
     for i, piece in enumerate(stacked):
         row = row + jnp.where(lane8 == sub8 + 8 * i, jnp.sum(piece, axis=1, keepdims=True), 0.0)
     row = jnp.sum(row, axis=0, keepdims=True)
+    part = [jnp.sum(powers[d][0:1], axis=1, keepdims=True) for d in range(2)]
+    row = jnp.concatenate([row, jnp.where(lane8[0:1] < SNRS, part[0], part[1])], axis=0)
     row_send[...] = row
     rows[freq] = row
 
@@ -318,12 +322,8 @@
 
     all_of(rows, n_freq - 1, 2).wait_recv()
     row = jnp.sum(rows[...], axis=0)
-    lane = lax.broadcasted_iota(jnp.int32, (1, LANES), 1)
-    power = [
-        jnp.sum(jnp.where(lane == 32 + d, row, 0.0), axis=1, keepdims=True) * (1.0 / (FOURIER_POINTS * RX * TX))
-        for d in range(2)
-    ]
-    weighted = row * jnp.where(lane < SNRS, power[0], jnp.where(lane < 2 * SNRS, power[1], 0.0))
+    powers_row = row[1:2] * (1.0 / (FOURIER_POINTS * RX * TX))
+    weighted = row[0:1] * powers_row
     sum_send[...] = weighted
     sums[drop] = weighted
 
@@ -339,6 +339,8 @@
     def _(i):
         copy_to({"drop": i}, sum_send, sums.at[drop], 3).start()
 
+    lane = lax.broadcasted_iota(jnp.int32, (1, LANES), 1)
+    power = [jnp.sum(jnp.where(lane == SNRS * d, powers_row, 0.0), axis=1, keepdims=True) for d in range(2)]
     for d in range(2):
         amplitude = std[d] * jnp.sqrt(jnp.broadcast_to(power[d], (8, LANES)))
         for t in range(TX):
@@ -400,14 +402,14 @@
             vmem((2 * SNRS * 2 * RX, LANES), F32),
             vmem((2 * SNRS * 8, LANES), F32),
             vmem((2 * SNRS * 8, LANES), jnp.bfloat16),
-            vmem((1, LANES), F32),
-            vmem((n_freq, 1, LANES), F32),
+            vmem((2, LANES), F32),
+            vmem((n_freq, 2, LANES), F32),
             vmem((1, LANES), F32),
             vmem((n_drop, 1, LANES), F32),
             pltpu.SemaphoreType.DMA((7,)),
             pltpu.SemaphoreType.DMA((4,)),
             pltpu.SemaphoreType.DMA((5,)),
-            pltpu.SemaphoreType.REGULAR((NY,)),
+            pltpu.SemaphoreType.REGULAR,
             pltpu.SemaphoreType.REGULAR,
         ],
         compiler_params=pltpu.CompilerParams(collective_id=0, has_side_effects=True, vmem_limit_bytes=16 << 20),

time: 33.9 us -> 33.9 us (level)
  no operation moved by 1% of the time
where the time goes in v6:
time: 33.9 us; the launch traced here: 33.8 us
  Pallas kernels  33.1 us (98%)
  between operations  0.64 us (2%)
    pallas_call x1, Pallas kernels, shards(): pl.pallas_call(kernel, out_shape=(jax.ShapeDtypeStruct((2 * SNRS * 8, LAN...  32.5 us

profile of v6, /device:TPU:1, one launch (start us, length us, event | category | flops | bytes accessed | tf_op | source)
XLA Modules:
  0.0 33.8 jit_solution(11914895446218916749)
XLA Ops:
  0.6 32.5 %shard_map.77 = (bf16[256,128]{1,0:T(8,128)(2,1)S(1)}, f32[1,16]{1,0:T(1,128)S(1)}) custom-call(f32[2,2,4,23]{3,2,1,0:T(4,128)} %bitcast.8, s32[2,23]{1,0:T(2,128)} %lags_hbm.1, f32[1,128]{1,0:T(1,128)} %bitcast.9, s32[128,128]{1,0:T(8,128)} %bitcast.7, bf16[2048,128]{1,0:T(8,128)(2,1)} %bitcast.6, f32[2,16]{1,0:T(2,128)} %std_hbm.1), custom_call_target="tpu_custom_call" | custom-call | tf_op jit(solution)/shard_map/pallas_call | solution.py:380
  33.1 0.7 %shard_map.78 = (bf16[256,128]{1,0:T(8,128)(2,1)}, f32[1,16]{1,0:T(1,128)}) custom-call(bf16[256,128]{1,0:T(8,128)(2,1)S(1)} %get-tuple-element.6.detected_ref, f32[1,16]{1,0:T(1,128)S(1)} %get-tuple-element.7.error_ref), custom_call_target="tpu_custom_call" | custom-call | tf_op jit(solution)/shard_map/pallas_call | solution.py:429
